TPU v7x, 256 devices: a whole 4x4x8 slice. The times are simulated.
256 devices in a mesh: term: 8 (over z), sec: 32 (over y, x, core).
Axes of the slice: x: 4, y: 4, z: 8, core: 2. Of those that a mesh axis runs over, the one named last changes fastest.
Arguments:
- start_vectors: bfloat16 [2, 64, 256, 256], P(None, 'sec'), may hold values from -6 to 6
- left_env: bfloat16 [32, 64, 256, 256], P('term', 'sec'), may hold values from -0.375 to 0.375
- right_env: bfloat16 [32, 64, 256, 256], P('term', 'sec'), may hold values from -0.375 to 0.375
- term_shift: int32 [32], P('term'), may hold values from -1 to 1
- precond: float32 [64, 256, 256], P('sec'), may hold values from 0.25 to 4
- block_dims: int32 [64], P('sec'), may hold values from 1 to 256, 8192 in all
Outputs:
- vector: float32 [2, 64, 256, 256], P(None, 'sec', 'term')
- energy: float32 [2], replicated
Inputs may be any that keep to these rules, and one draw needn't show every extreme that they name: `block_dims`: one block has exactly 256 live states.
All inputs are finite; a program needn't handle non-finite values.
Results may differ from a plain program's by a relative error of at most 0.0036.
Values may be sent and summed in bfloat16 or wider, within the bound.
No kernel may reach another device: no remote copies, remote signals or barrier semaphores. Data moves between devices by JAX's collectives and lax.ppermute only.
A program may use at most 64 MiB of HBM per device.

v0:
```python
import jax
import jax.numpy as jnp
from jax import lax
from jax.sharding import PartitionSpec as P

ITERS = 2


def padded(x, sides, width):
    for axis, dim in sides:
        count, length = (lax.axis_size(axis), x.shape[dim])
        up = [(i, (i + 1) % count) for i in range(count - 1)]
        down = [(j, i) for i, j in up]
        last = lax.slice_in_dim(x, length - width, length, axis=dim)
        initial = lax.slice_in_dim(x, 0, width, axis=dim)
        before = lax.ppermute(last, axis, up)
        after = lax.ppermute(initial, axis, down)
        x = jnp.concatenate([before, x, after], axis=dim)
    return x


def shards(start_vectors, left_env, right_env, term_shift, precond, block_dims):
    vec_count, blocks, states, _ = start_vectors.shape
    groups = lax.axis_size("term")
    share = states // groups
    offset_row = lax.axis_index("term") * share
    factor = 1.0 / (blocks * lax.axis_size("sec") * states * states)
    position = jnp.arange(states, dtype=jnp.int32)
    live_rows = position[None, :, None] < block_dims[:, None, None]
    live_cols = position[None, None, :] < block_dims[:, None, None]
    mask = (live_rows & live_cols).astype(jnp.float32)
    shift_sel = term_shift[:, None, None, None, None]

    def apply_op(vector_bf):
        local = jnp.einsum(
            "ujab,kjcb->kujac", vector_bf, right_env, preferred_element_type=jnp.float32
        ).astype(jnp.bfloat16)
        wide = padded(local, (("sec", 2),), 1)
        chosen = jnp.where(
            shift_sel < 0,
            wide[:, :, 0:blocks],
            jnp.where(shift_sel == 0, wide[:, :, 1 : blocks + 1], wide[:, :, 2 : blocks + 2]),
        )
        partial_sum = (
            jnp.einsum("kbac,kubcd->ubad", left_env, chosen, preferred_element_type=jnp.float32)
            * mask
        )
        result = lax.psum(partial_sum, "term")
        return result

    def totals(values):
        result = lax.psum(values, "sec")
        return result

    def inner(left, right):
        return jnp.sum(left * right, axis=(1, 2, 3)) * factor

    def expand(value):
        return value[:, None, None, None]

    start = start_vectors * mask.astype(jnp.bfloat16)
    h_vec = apply_op(start)
    vector = start.astype(jnp.float32)
    pre_view = precond[None]
    length = jnp.sqrt(totals(inner(vector, vector)[None])[0] + 1e-06)
    vector = vector / expand(length)
    h_vec = h_vec / expand(length)
    energy = jnp.zeros((vec_count,), jnp.float32)
    for iteration in range(ITERS):
        rayleigh = totals(inner(vector, h_vec)[None])[0]
        resid = h_vec - expand(rayleigh) * vector
        precon_res = pre_view * resid
        correlation = totals(inner(vector, precon_res)[None])[0]
        direction = precon_res - expand(correlation) * vector
        pair = totals(jnp.stack([inner(direction, direction), inner(direction, h_vec)]))
        square, raw_coupling = (pair[0], pair[1])
        dir_norm = jnp.sqrt(square + 1e-06)
        coupling = raw_coupling / dir_norm
        direction = direction / expand(dir_norm)
        widen_result = direction.astype(jnp.bfloat16)
        h_dir = apply_op(widen_result)
        curvature = totals(inner(direction, h_dir)[None])[0]
        energy = 0.5 * (rayleigh + curvature) - jnp.sqrt(
            (0.5 * (rayleigh - curvature)) ** 2 + coupling**2
        )
        weight = energy - rayleigh
        new_size = jnp.sqrt(coupling**2 + weight**2)
        vector = (expand(coupling) * vector + expand(weight) * direction) / expand(new_size)
        h_vec = (expand(coupling) * h_vec + expand(weight) * h_dir) / expand(new_size)
    final = lax.dynamic_slice_in_dim(vector, offset_row, share, 2)
    return (final, energy)


def solution(mesh):
    return jax.shard_map(
        shards,
        mesh=mesh,
        in_specs=(
            P(None, "sec", None, None),
            P("term", "sec", None, None),
            P("term", "sec", None, None),
            P("term"),
            P("sec", None, None),
            P("sec"),
        ),
        out_specs=(P(None, "sec", "term", None), P()),
        check_vma=False,
    )
```

profile of v0, /device:TPU:1, one launch (start us, length us, event | category | flops | bytes accessed | tf_op | source)
XLA Modules:
  0.0 827.7 jit_solution(5210906045877564215)
XLA Ops:
  10.7 4.6 collective-permute-start
  15.3 2.0 collective-permute-start.1
  17.3 9.7 %collective-permute-done = bf16[4,2,1,256,256]{4,3,0,1,2:T(8,128)(2,1)S(1)} collective-permute-done((bf16[4,2,1,256,256]{4,3,0,1,2:T(8,128)(2,1)S(1)}, bf16[4,2,1,256,256]{4,3,0,1,2:T(8,128)(2,1)S(1)}, u32[]{:S(2)}, u32[]{:S(2)}) %collective-permute-start) | collective-permute-done | bytes 1048608 | tf_op jit(solution)/shard_map/ppermute | solution.py:16
  27.1 4.4 collective-permute-done.1
  31.5 2.4 fusion.27
  34.3 61.0 %psum.85 = f32[1,2]{1,0:T(1,128)S(1)} all-reduce(f32[1,2]{1,0:T(1,128)S(1)} %multiply_bitcast_fusion.6), channel_id=1, replica_groups=mesh['term'=8,'sec'=32] {'sec'}, use_global_device_ids=true, to_apply=%region_2.3 | all-reduce | flops 2 | bytes 16 | tf_op jit(solution)/shard_map/psum | solution.py:52
  95.3 14.4 %all-reduce.4.cloned.1.call-done = f32[2,2,256,256]{2,3,0,1:T(8,128)} async-done(((f32[2,2,256,256]{2,3,0,1:T(8,128)}), f32[2,2,256,256]{2,3,0,1:T(8,128)}) %all-reduce.4.cloned.1.call-update) | async-done | bytes 1048592 | tf_op jit(solution)/shard_map/psum | solution.py:48
  112.6 67.1 %psum.86 = f32[2]{0:T(128)S(1)} all-reduce(f32[2]{0:T(128)S(1)} %broadcast_multiply_fusion.5), channel_id=1, replica_groups=mesh['term'=8,'sec'=32] {'sec'}, use_global_device_ids=true, to_apply=%region_4.5 | all-reduce | flops 2 | bytes 16 | tf_op jit(solution)/shard_map/psum | solution.py:52
  180.2 62.7 %psum.87 = f32[2]{0:T(128)S(1)} all-reduce(f32[2]{0:T(128)S(1)} %broadcast_multiply_fusion.4), channel_id=1, replica_groups=mesh['term'=8,'sec'=32] {'sec'}, use_global_device_ids=true, to_apply=%region_6.7 | all-reduce | flops 2 | bytes 16 | tf_op jit(solution)/shard_map/psum | solution.py:52
  244.5 62.7 %psum.88 = f32[2,2]{1,0:T(2,128)S(1)} all-reduce(f32[2,2]{1,0:T(2,128)S(1)} %pad_maximum_fusion.9), channel_id=1, replica_groups=mesh['term'=8,'sec'=32] {'sec'}, use_global_device_ids=true, to_apply=%region_9.10 | all-reduce | flops 4 | bytes 32 | tf_op jit(solution)/shard_map/psum | solution.py:52
  307.2 2.1 convert_bitcast_fusion.1
  309.5 2.1 collective-permute-start.2
  311.6 2.5 collective-permute-start.3
  314.0 9.2 %collective-permute-done.2 = bf16[4,2,1,256,256]{4,3,0,1,2:T(8,128)(2,1)S(1)} collective-permute-done((bf16[4,2,1,256,256]{4,3,0,1,2:T(8,128)(2,1)S(1)}, bf16[4,2,1,256,256]{4,3,0,1,2:T(8,128)(2,1)S(1)}, u32[]{:S(2)}, u32[]{:S(2)}) %collective-permute-start.2) | collective-permute-done | bytes 1048608 | tf_op jit(solution)/shard_map/ppermute | solution.py:16
  323.3 4.4 collective-permute-done.3
  327.7 2.4 fusion.33
  330.1 65.6 %all-reduce.6.cloned.1.call-done = f32[2,2,256,256]{2,3,0,1:T(8,128)} async-done(((f32[2,2,256,256]{2,3,0,1:T(8,128)}), f32[2,2,256,256]{2,3,0,1:T(8,128)}) %all-reduce.6.cloned.1.call-update) | async-done | bytes 1048592 | tf_op jit(solution)/shard_map/psum | solution.py:48
  397.7 67.1 %psum.90 = f32[2]{0:T(128)S(1)} all-reduce(f32[2]{0:T(128)S(1)} %broadcast_multiply_fusion.3), channel_id=1, replica_groups=mesh['term'=8,'sec'=32] {'sec'}, use_global_device_ids=true, to_apply=%region_12.13 | all-reduce | flops 2 | bytes 16 | tf_op jit(solution)/shard_map/psum | solution.py:52
  464.8 3.5 multiply_reduce_fusion.4
  468.3 62.8 %psum.91 = f32[2]{0:T(128)S(1)} all-reduce(f32[2]{0:T(128)S(1)} %broadcast_multiply_fusion.2), channel_id=1, replica_groups=mesh['term'=8,'sec'=32] {'sec'}, use_global_device_ids=true, to_apply=%region_14.15 | all-reduce | flops 2 | bytes 16 | tf_op jit(solution)/shard_map/psum | solution.py:52
  531.1 1.9 multiply_reduce_fusion.3
  533.0 62.7 %psum.92 = f32[2]{0:T(128)S(1)} all-reduce(f32[2]{0:T(128)S(1)} %broadcast_multiply_fusion.1), channel_id=1, replica_groups=mesh['term'=8,'sec'=32] {'sec'}, use_global_device_ids=true, to_apply=%region_16.17 | all-reduce | flops 2 | bytes 16 | tf_op jit(solution)/shard_map/psum | solution.py:52
  595.6 2.6 multiply_reduce_fusion.2
  598.2 62.7 %psum.93 = f32[2,2]{1,0:T(2,128)S(1)} all-reduce(f32[2,2]{1,0:T(2,128)S(1)} %pad_maximum_fusion.10), channel_id=1, replica_groups=mesh['term'=8,'sec'=32] {'sec'}, use_global_device_ids=true, to_apply=%region_19.20 | all-reduce | flops 4 | bytes 32 | tf_op jit(solution)/shard_map/psum | solution.py:52
  663.5 2.1 collective-permute-start.4
  665.6 2.5 collective-permute-start.5
  668.1 9.2 %collective-permute-done.4 = bf16[4,2,1,256,256]{4,3,0,1,2:T(8,128)(2,1)S(1)} collective-permute-done((bf16[4,2,1,256,256]{4,3,0,1,2:T(8,128)(2,1)S(1)}, bf16[4,2,1,256,256]{4,3,0,1,2:T(8,128)(2,1)S(1)}, u32[]{:S(2)}, u32[]{:S(2)}) %collective-permute-start.4) | collective-permute-done | bytes 1048608 | tf_op jit(solution)/shard_map/ppermute | solution.py:16
  677.3 4.4 collective-permute-done.5
  681.7 2.4 fusion.39
  684.1 65.3 %all-reduce.8.cloned.1.call-done = f32[2,2,256,256]{2,3,0,1:T(8,128)} async-done(((f32[2,2,256,256]{2,3,0,1:T(8,128)}), f32[2,2,256,256]{2,3,0,1:T(8,128)}) %all-reduce.8.cloned.1.call-update) | async-done | bytes 1048592 | tf_op jit(solution)/shard_map/psum | solution.py:48
  749.4 1.9 multiply_reduce_fusion
  751.3 67.1 %psum.95 = f32[2]{0:T(128)S(1)} all-reduce(f32[2]{0:T(128)S(1)} %broadcast_multiply_fusion), channel_id=1, replica_groups=mesh['term'=8,'sec'=32] {'sec'}, use_global_device_ids=true, to_apply=%region_22.23 | all-reduce | flops 2 | bytes 16 | tf_op jit(solution)/shard_map/psum | solution.py:52
  (63 shorter events, 16.4 us)
Async XLA Ops:
  7.2 2.5 copy-start
  7.2 102.5 %all-reduce.4.cloned.1.call-start = ((), (), s32[]{:S(2)}) async-start(), calls=%async_computation | async-start | bytes 2097152 | tf_op jit(solution)/shard_map/psum | solution.py:48
  8.2 23.3 %copy-start.4 = (f32[2,256,256]{1,2,0:T(8,128)}, f32[2,256,256]{1,2,0:T(8,128)S(1)}, u32[]{:S(2)}) copy-start(f32[2,256,256]{1,2,0:T(8,128)S(1)} %get-tuple-element.26) | copy-start | bytes 1572868
  10.5 6.8 copy-start.10
  10.5 21.0 %copy-start.7 = (bf16[4,2,256,256]{3,2,1,0:T(8,128)(2,1)S(1)}, bf16[4,2,256,256]{3,2,1,0:T(8,128)(2,1)}, u32[]{:S(2)}) copy-start(bf16[4,2,256,256]{3,2,1,0:T(8,128)(2,1)} %param.7) | copy-start | bytes 3145732
  10.7 16.4 %collective-permute-start = (bf16[4,2,1,256,256]{4,3,0,1,2:T(8,128)(2,1)S(1)}, bf16[4,2,1,256,256]{4,3,0,1,2:T(8,128)(2,1)S(1)}, u32[]{:S(2)}, u32[]{:S(2)}) collective-permute-start(bf16[4,2,1,256,256]{4,3,0,1,2:T(8,128)(2,1)S(1)} %get-tuple-element.24), channel_id=1, source_target_pairs={{0,1},{1,2},{2,3},{3,4},{4,5},{5,6},{6,7},{7,8},{8,9},{9,10},{10,1... | collective-permute-start | bytes 3145736 | tf_op jit(solution)/shard_map/ppermute | solution.py:16
  15.3 16.1 %collective-permute-start.1 = (bf16[4,2,1,256,256]{4,3,0,1,2:T(8,128)(2,1)S(1)}, bf16[4,2,1,256,256]{4,3,0,1,2:T(8,128)(2,1)S(1)}, u32[]{:S(2)}, u32[]{:S(2)}) collective-permute-start(bf16[4,2,1,256,256]{4,3,0,1,2:T(8,128)(2,1)S(1)} %get-tuple-element.25), channel_id=1, source_target_pairs={{1,0},{2,1},{3,2},{4,3},{5,4},{6,5},{7,6},{8,7},{9,8},{10,9},{11,1... | collective-permute-start | bytes 3145736 | tf_op jit(solution)/shard_map/ppermute | solution.py:17
  33.9 361.9 %all-reduce.6.cloned.1.call-start = ((), (), s32[]{:S(2)}) async-start(), calls=%async_computation.1 | async-start | bytes 2097152 | tf_op jit(solution)/shard_map/psum | solution.py:48
  109.7 70.1 %copy-start.1 = (f32[2,2,256,256]{2,3,0,1:T(8,128)S(1)}, f32[2,2,256,256]{2,3,0,1:T(8,128)}, u32[]{:S(2)}) copy-start(f32[2,2,256,256]{2,3,0,1:T(8,128)} %all-reduce.4.cloned.1.call-done) | copy-start | bytes 3145732
  309.3 18.4 %copy-start.5 = (f32[2,256,256]{1,2,0:T(8,128)S(1)}, f32[2,256,256]{1,2,0:T(8,128)}, u32[]{:S(2)}) copy-start(f32[2,256,256]{1,2,0:T(8,128)} %copy-done.4) | copy-start | bytes 1572868
  309.3 18.4 %copy-start.8 = (bf16[4,2,256,256]{3,2,1,0:T(8,128)(2,1)S(1)}, bf16[4,2,256,256]{3,2,1,0:T(8,128)(2,1)}, u32[]{:S(2)}) copy-start(bf16[4,2,256,256]{3,2,1,0:T(8,128)(2,1)} %param.7) | copy-start | bytes 3145732
  309.5 13.8 %collective-permute-start.2 = (bf16[4,2,1,256,256]{4,3,0,1,2:T(8,128)(2,1)S(1)}, bf16[4,2,1,256,256]{4,3,0,1,2:T(8,128)(2,1)S(1)}, u32[]{:S(2)}, u32[]{:S(2)}) collective-permute-start(bf16[4,2,1,256,256]{4,3,0,1,2:T(8,128)(2,1)S(1)} %get-tuple-element.22), channel_id=1, source_target_pairs={{0,1},{1,2},{2,3},{3,4},{4,5},{5,6},{6,7},{7,8},{8,9},{9,10},{10,1... | collective-permute-start | bytes 3145736 | tf_op jit(solution)/shard_map/ppermute | solution.py:16
  311.6 16.1 %collective-permute-start.3 = (bf16[4,2,1,256,256]{4,3,0,1,2:T(8,128)(2,1)S(1)}, bf16[4,2,1,256,256]{4,3,0,1,2:T(8,128)(2,1)S(1)}, u32[]{:S(2)}, u32[]{:S(2)}) collective-permute-start(bf16[4,2,1,256,256]{4,3,0,1,2:T(8,128)(2,1)S(1)} %get-tuple-element.23), channel_id=1, source_target_pairs={{1,0},{2,1},{3,2},{4,3},{5,4},{6,5},{7,6},{8,7},{9,8},{10,9},{11,1... | collective-permute-start | bytes 3145736 | tf_op jit(solution)/shard_map/ppermute | solution.py:17
  330.1 419.3 %all-reduce.8.cloned.1.call-start = ((), (), s32[]{:S(2)}) async-start(), calls=%async_computation.2 | async-start | bytes 2097152 | tf_op jit(solution)/shard_map/psum | solution.py:48
  468.3 127.4 %copy-start.2 = (f32[2,2,256,256]{2,3,0,1:T(8,128)S(1)}, f32[2,2,256,256]{2,3,0,1:T(8,128)}, u32[]{:S(2)}) copy-start(f32[2,2,256,256]{2,3,0,1:T(8,128)} %get-tuple-element.15) | copy-start | bytes 3145732
  662.3 1.0 copy-start.3
  663.4 18.4 %copy-start.6 = (f32[2,256,256]{1,2,0:T(8,128)S(1)}, f32[2,256,256]{1,2,0:T(8,128)}, u32[]{:S(2)}) copy-start(f32[2,256,256]{1,2,0:T(8,128)} %copy-done.4) | copy-start | bytes 1572868
  663.4 18.4 %copy-start.9 = (bf16[4,2,256,256]{3,2,1,0:T(8,128)(2,1)S(1)}, bf16[4,2,256,256]{3,2,1,0:T(8,128)(2,1)}, u32[]{:S(2)}) copy-start(bf16[4,2,256,256]{3,2,1,0:T(8,128)(2,1)} %param.7) | copy-start | bytes 3145732
  663.5 13.8 %collective-permute-start.4 = (bf16[4,2,1,256,256]{4,3,0,1,2:T(8,128)(2,1)S(1)}, bf16[4,2,1,256,256]{4,3,0,1,2:T(8,128)(2,1)S(1)}, u32[]{:S(2)}, u32[]{:S(2)}) collective-permute-start(bf16[4,2,1,256,256]{4,3,0,1,2:T(8,128)(2,1)S(1)} %get-tuple-element.20), channel_id=1, source_target_pairs={{0,1},{1,2},{2,3},{3,4},{4,5},{5,6},{6,7},{7,8},{8,9},{9,10},{10,1... | collective-permute-start | bytes 3145736 | tf_op jit(solution)/shard_map/ppermute | solution.py:16
  665.6 16.1 %collective-permute-start.5 = (bf16[4,2,1,256,256]{4,3,0,1,2:T(8,128)(2,1)S(1)}, bf16[4,2,1,256,256]{4,3,0,1,2:T(8,128)(2,1)S(1)}, u32[]{:S(2)}, u32[]{:S(2)}) collective-permute-start(bf16[4,2,1,256,256]{4,3,0,1,2:T(8,128)(2,1)S(1)} %get-tuple-element.21), channel_id=1, source_target_pairs={{1,0},{2,1},{3,2},{4,3},{5,4},{6,5},{7,6},{8,7},{9,8},{10,9},{11,1... | collective-permute-start | bytes 3145736 | tf_op jit(solution)/shard_map/ppermute | solution.py:17
Sparse Core Ops, SparseCore 0:
  34.0 75.5 all-reduce.3
  330.2 65.5 all-reduce.5
  684.2 65.1 all-reduce.7
where the time goes:
time: 829 us; the launch traced here: 828 us
  blocking collectives  576 us (69%)
  waiting for transfers between devices  187 us (23%)
  other arithmetic  20.1 us (2%)
  starting transfers between devices  15.8 us (2%)
  between operations  14 us (2%)
  matrix products  11 us (1%)
    psum x9, blocking collectives, totals(): result = lax.psum(values, 'sec')  576 us
    psum x3, waiting for transfers between devices, apply_op(): result = lax.psum(partial_sum, 'term')  145 us
    ppermute x3, waiting for transfers between devices, padded(): before = lax.ppermute(last, axis, up)  28.2 us
  transfers between devices with their start and end apart: 9, of which 9 were waited for; matrix products, arithmetic and copies ran while one was open for 0% of the time, Pallas kernels for 0%

commit v1 on v0

--- a/solution.py
+++ b/solution.py
@@ -49,7 +49,9 @@
         return result
 
     def totals(values):
-        result = lax.psum(values, "sec")
+        result = values
+        for hop in (1, 2, 4, 8, 16):
+            result = result + lax.ppermute(result, "sec", [(dev, dev ^ hop) for dev in range(32)])
         return result
 
     def inner(left, right):

time: 829 us -> 487 us (0.59)
  the two profiles are of different devices: /device:TPU:1 before, /device:TPU:2 now
where the time goes in v1:
time: 487 us; the launch traced here: 478 us
  waiting for transfers between devices  352 us (72%)
  starting transfers between devices  86.8 us (18%)
  between operations  14.5 us (3%)
  other arithmetic  11.4 us (2%)
  matrix products  9.71 us (2%)
    psum x3, waiting for transfers between devices, apply_op(): result = lax.psum(partial_sum, 'term')  216 us
    ppermute x45, waiting for transfers between devices, totals(): lax.ppermute(result, 'sec', [(dev, dev ^ hop) for dev in range(32)])  99.4 us
    ppermute x45, starting transfers between devices, totals(): lax.ppermute(result, 'sec', [(dev, dev ^ hop) for dev in range(32)])  69.5 us
    ppermute x3, waiting for transfers between devices, padded(): before = lax.ppermute(last, axis, up)  31.6 us
    ppermute x3, starting transfers between devices, padded(): after = lax.ppermute(initial, axis, down)  10.9 us
  transfers between devices with their start and end apart: 54, of which 54 were waited for; matrix products, arithmetic and copies ran while one was open for 0% of the time, Pallas kernels for 0%

profile of v1, /device:TPU:2, one launch (start us, length us, event | category | flops | bytes accessed | tf_op | source)
XLA Modules:
  0.0 478.0 jit_solution(5922897029188140077)
XLA Ops:
  12.8 3.6 collective-permute-start.1
  16.4 10.5 %collective-permute-done = bf16[4,2,1,256,256]{4,3,0,1,2:T(8,128)(2,1)S(1)} collective-permute-done((bf16[4,2,1,256,256]{4,3,0,1,2:T(8,128)(2,1)S(1)}, bf16[4,2,1,256,256]{4,3,0,1,2:T(8,128)(2,1)S(1)}, u32[]{:S(2)}, u32[]{:S(2)}) %collective-permute-start) | collective-permute-done | bytes 1048608 | tf_op jit(solution)/shard_map/ppermute | solution.py:16
  34.6 3.0 collective-permute-done.3
  37.7 4.2 collective-permute-start.4
  52.1 61.1 %all-reduce.4.cloned.1.call-done = f32[2,2,256,256]{2,3,0,1:T(8,128)} async-done(((f32[2,2,256,256]{2,3,0,1:T(8,128)}), f32[2,2,256,256]{2,3,0,1:T(8,128)}) %all-reduce.4.cloned.1.call-update) | async-done | bytes 1048592 | tf_op jit(solution)/shard_map/psum | solution.py:48
  116.6 3.0 collective-permute-done.8
  121.7 3.0 collective-permute-done.9
  128.3 3.0 collective-permute-start.11
  135.6 3.0 collective-permute-done.13
  140.7 3.0 collective-permute-done.14
  147.4 3.0 collective-permute-start.16
  155.3 3.0 collective-permute-done.18
  160.4 3.0 collective-permute-done.19
  167.0 3.0 collective-permute-start.21
  175.3 3.6 collective-permute-start.23
  178.9 10.5 %collective-permute-done.22 = bf16[4,2,1,256,256]{4,3,0,1,2:T(8,128)(2,1)S(1)} collective-permute-done((bf16[4,2,1,256,256]{4,3,0,1,2:T(8,128)(2,1)S(1)}, bf16[4,2,1,256,256]{4,3,0,1,2:T(8,128)(2,1)S(1)}, u32[]{:S(2)}, u32[]{:S(2)}) %collective-permute-start.22) | collective-permute-done | bytes 1048608 | tf_op jit(solution)/shard_map/ppermute | solution.py:16
  193.7 77.5 %all-reduce.6.cloned.1.call-done = f32[2,2,256,256]{2,3,0,1:T(8,128)} async-done(((f32[2,2,256,256]{2,3,0,1:T(8,128)}), f32[2,2,256,256]{2,3,0,1:T(8,128)}) %all-reduce.6.cloned.1.call-update) | async-done | bytes 1048592 | tf_op jit(solution)/shard_map/psum | solution.py:48
  280.1 3.0 collective-permute-done.26
  286.7 3.0 collective-permute-start.28
  299.7 3.0 collective-permute-done.31
  306.3 3.0 collective-permute-start.33
  318.7 3.0 collective-permute-done.36
  325.3 3.0 collective-permute-start.38
  333.1 3.0 collective-permute-done.40
  338.2 3.0 collective-permute-done.41
  344.8 3.0 collective-permute-start.43
  353.3 3.6 collective-permute-start.45
  357.0 10.5 %collective-permute-done.44 = bf16[4,2,1,256,256]{4,3,0,1,2:T(8,128)(2,1)S(1)} collective-permute-done((bf16[4,2,1,256,256]{4,3,0,1,2:T(8,128)(2,1)S(1)}, bf16[4,2,1,256,256]{4,3,0,1,2:T(8,128)(2,1)S(1)}, u32[]{:S(2)}, u32[]{:S(2)}) %collective-permute-start.44) | collective-permute-done | bytes 1048608 | tf_op jit(solution)/shard_map/ppermute | solution.py:16
  371.7 77.5 %all-reduce.8.cloned.1.call-done = f32[2,2,256,256]{2,3,0,1:T(8,128)} async-done(((f32[2,2,256,256]{2,3,0,1:T(8,128)}), f32[2,2,256,256]{2,3,0,1:T(8,128)}) %all-reduce.8.cloned.1.call-update) | async-done | bytes 1048592 | tf_op jit(solution)/shard_map/psum | solution.py:48
  452.7 3.0 collective-permute-done.47
  457.7 3.0 collective-permute-done.48
  464.3 3.0 collective-permute-start.50
  (198 shorter events, 134.7 us)
Async XLA Ops:
  7.2 106.0 %all-reduce.4.cloned.1.call-start = ((), (), s32[]{:S(2)}) async-start(), calls=%async_computation | async-start | bytes 2097152 | tf_op jit(solution)/shard_map/psum | solution.py:48
  10.7 16.2 %collective-permute-start = (bf16[4,2,1,256,256]{4,3,0,1,2:T(8,128)(2,1)S(1)}, bf16[4,2,1,256,256]{4,3,0,1,2:T(8,128)(2,1)S(1)}, u32[]{:S(2)}, u32[]{:S(2)}) collective-permute-start(bf16[4,2,1,256,256]{4,3,0,1,2:T(8,128)(2,1)S(1)} %get-tuple-element.24), channel_id=1, source_target_pairs={{0,1},{1,2},{2,3},{3,4},{4,5},{5,6},{6,7},{7,8},{8,9},{9,10},{10,1... | collective-permute-start | bytes 3145736 | tf_op jit(solution)/shard_map/ppermute | solution.py:16
  12.8 15.9 %collective-permute-start.1 = (bf16[4,2,1,256,256]{4,3,0,1,2:T(8,128)(2,1)S(1)}, bf16[4,2,1,256,256]{4,3,0,1,2:T(8,128)(2,1)S(1)}, u32[]{:S(2)}, u32[]{:S(2)}) collective-permute-start(bf16[4,2,1,256,256]{4,3,0,1,2:T(8,128)(2,1)S(1)} %get-tuple-element.25), channel_id=1, source_target_pairs={{1,0},{2,1},{3,2},{4,3},{5,4},{6,5},{7,6},{8,7},{9,8},{10,9},{11,1... | collective-permute-start | bytes 3145736 | tf_op jit(solution)/shard_map/ppermute | solution.py:17
  31.1 240.1 %all-reduce.6.cloned.1.call-start = ((), (), s32[]{:S(2)}) async-start(), calls=%async_computation.1 | async-start | bytes 2097152 | tf_op jit(solution)/shard_map/psum | solution.py:48
  37.7 5.8 %collective-permute-start.4 = (f32[1,2]{1,0:T(1,128)S(1)}, f32[1,2]{1,0:T(1,128)S(1)}, u32[]{:S(2)}, u32[]{:S(2)}) collective-permute-start(f32[1,2]{1,0:T(1,128)S(1)} %add.250), channel_id=1, source_target_pairs={{0,4},{1,5},{2,6},{3,7},{4,0},{5,1},{6,2},{7,3},{8,12},{9,13},{10,... | collective-permute-start | bytes 32 | tf_op jit(solution)/shard_map/ppermute | solution.py:54
  47.0 5.1 %collective-permute-start.6 = (f32[1,2]{1,0:T(1,128)S(1)}, f32[1,2]{1,0:T(1,128)S(1)}, u32[]{:S(2)}, u32[]{:S(2)}) collective-permute-start(f32[1,2]{1,0:T(1,128)S(1)} %add.252), channel_id=1, source_target_pairs={{0,16},{1,17},{2,18},{3,19},{4,20},{5,21},{6,22},{7,23},{8,24},{9,... | collective-permute-start | bytes 32 | tf_op jit(solution)/shard_map/ppermute | solution.py:54
  119.6 5.1 %collective-permute-start.9 = (f32[1,2]{1,0:T(1,128)S(1)}, f32[1,2]{1,0:T(1,128)S(1)}, u32[]{:S(2)}, u32[]{:S(2)}) collective-permute-start(f32[1,2]{1,0:T(1,128)S(1)} %add.256), channel_id=1, source_target_pairs={{0,4},{1,5},{2,6},{3,7},{4,0},{5,1},{6,2},{7,3},{8,12},{9,13},{10,... | collective-permute-start | bytes 32 | tf_op jit(solution)/shard_map/ppermute | solution.py:54
  128.3 5.1 %collective-permute-start.11 = (f32[1,2]{1,0:T(1,128)S(1)}, f32[1,2]{1,0:T(1,128)S(1)}, u32[]{:S(2)}, u32[]{:S(2)}) collective-permute-start(f32[1,2]{1,0:T(1,128)S(1)} %add.258), channel_id=1, source_target_pairs={{0,16},{1,17},{2,18},{3,19},{4,20},{5,21},{6,22},{7,23},{8,24},{9,... | collective-permute-start | bytes 32 | tf_op jit(solution)/shard_map/ppermute | solution.py:54
  138.6 5.1 %collective-permute-start.14 = (f32[1,2]{1,0:T(1,128)S(1)}, f32[1,2]{1,0:T(1,128)S(1)}, u32[]{:S(2)}, u32[]{:S(2)}) collective-permute-start(f32[1,2]{1,0:T(1,128)S(1)} %add.261), channel_id=1, source_target_pairs={{0,4},{1,5},{2,6},{3,7},{4,0},{5,1},{6,2},{7,3},{8,12},{9,13},{10,... | collective-permute-start | bytes 32 | tf_op jit(solution)/shard_map/ppermute | solution.py:54
  143.7 3.7 collective-permute-start.15
  147.4 5.1 %collective-permute-start.16 = (f32[1,2]{1,0:T(1,128)S(1)}, f32[1,2]{1,0:T(1,128)S(1)}, u32[]{:S(2)}, u32[]{:S(2)}) collective-permute-start(f32[1,2]{1,0:T(1,128)S(1)} %add.263), channel_id=1, source_target_pairs={{0,16},{1,17},{2,18},{3,19},{4,20},{5,21},{6,22},{7,23},{8,24},{9,... | collective-permute-start | bytes 32 | tf_op jit(solution)/shard_map/ppermute | solution.py:54
  154.6 3.7 collective-permute-start.18
  158.3 5.2 %collective-permute-start.19 = (f32[2,2]{1,0:T(2,128)S(1)}, f32[2,2]{1,0:T(2,128)S(1)}, u32[]{:S(2)}, u32[]{:S(2)}) collective-permute-start(f32[2,2]{1,0:T(2,128)S(1)} %fusion.88), channel_id=1, source_target_pairs={{0,4},{1,5},{2,6},{3,7},{4,0},{5,1},{6,2},{7,3},{8,12},{9,13},{10,... | collective-permute-start | bytes 56 | tf_op jit(solution)/shard_map/ppermute | solution.py:54
  163.4 3.6 collective-permute-start.20
  167.0 5.1 %collective-permute-start.21 = (f32[2,2]{1,0:T(2,128)S(1)}, f32[2,2]{1,0:T(2,128)S(1)}, u32[]{:S(2)}, u32[]{:S(2)}) collective-permute-start(f32[2,2]{1,0:T(2,128)S(1)} %add.268), channel_id=1, source_target_pairs={{0,16},{1,17},{2,18},{3,19},{4,20},{5,21},{6,22},{7,23},{8,24},{9,... | collective-permute-start | bytes 56 | tf_op jit(solution)/shard_map/ppermute | solution.py:54
  173.2 16.2 %collective-permute-start.22 = (bf16[4,2,1,256,256]{4,3,0,1,2:T(8,128)(2,1)S(1)}, bf16[4,2,1,256,256]{4,3,0,1,2:T(8,128)(2,1)S(1)}, u32[]{:S(2)}, u32[]{:S(2)}) collective-permute-start(bf16[4,2,1,256,256]{4,3,0,1,2:T(8,128)(2,1)S(1)} %get-tuple-element.22), channel_id=1, source_target_pairs={{0,1},{1,2},{2,3},{3,4},{4,5},{5,6},{6,7},{7,8},{8,9},{9,10},{10,1... | collective-permute-start | bytes 3145736 | tf_op jit(solution)/shard_map/ppermute | solution.py:16
  175.3 15.9 %collective-permute-start.23 = (bf16[4,2,1,256,256]{4,3,0,1,2:T(8,128)(2,1)S(1)}, bf16[4,2,1,256,256]{4,3,0,1,2:T(8,128)(2,1)S(1)}, u32[]{:S(2)}, u32[]{:S(2)}) collective-permute-start(bf16[4,2,1,256,256]{4,3,0,1,2:T(8,128)(2,1)S(1)} %get-tuple-element.23), channel_id=1, source_target_pairs={{1,0},{2,1},{3,2},{4,3},{5,4},{6,5},{7,6},{8,7},{9,8},{10,9},{11,1... | collective-permute-start | bytes 3145736 | tf_op jit(solution)/shard_map/ppermute | solution.py:17
  193.6 255.6 %all-reduce.8.cloned.1.call-start = ((), (), s32[]{:S(2)}) async-start(), calls=%async_computation.2 | async-start | bytes 2097152 | tf_op jit(solution)/shard_map/psum | solution.py:48
  278.0 5.1 %collective-permute-start.26 = (f32[1,2]{1,0:T(1,128)S(1)}, f32[1,2]{1,0:T(1,128)S(1)}, u32[]{:S(2)}, u32[]{:S(2)}) collective-permute-start(f32[1,2]{1,0:T(1,128)S(1)} %add.272), channel_id=1, source_target_pairs={{0,4},{1,5},{2,6},{3,7},{4,0},{5,1},{6,2},{7,3},{8,12},{9,13},{10,... | collective-permute-start | bytes 32 | tf_op jit(solution)/shard_map/ppermute | solution.py:54
  286.7 5.1 %collective-permute-start.28 = (f32[1,2]{1,0:T(1,128)S(1)}, f32[1,2]{1,0:T(1,128)S(1)}, u32[]{:S(2)}, u32[]{:S(2)}) collective-permute-start(f32[1,2]{1,0:T(1,128)S(1)} %add.274), channel_id=1, source_target_pairs={{0,16},{1,17},{2,18},{3,19},{4,20},{5,21},{6,22},{7,23},{8,24},{9,... | collective-permute-start | bytes 32 | tf_op jit(solution)/shard_map/ppermute | solution.py:54
  297.5 5.3 %collective-permute-start.31 = (f32[1,2]{1,0:T(1,128)S(1)}, f32[1,2]{1,0:T(1,128)S(1)}, u32[]{:S(2)}, u32[]{:S(2)}) collective-permute-start(f32[1,2]{1,0:T(1,128)S(1)} %add.282), channel_id=1, source_target_pairs={{0,4},{1,5},{2,6},{3,7},{4,0},{5,1},{6,2},{7,3},{8,12},{9,13},{10,... | collective-permute-start | bytes 32 | tf_op jit(solution)/shard_map/ppermute | solution.py:54
  306.3 5.1 %collective-permute-start.33 = (f32[1,2]{1,0:T(1,128)S(1)}, f32[1,2]{1,0:T(1,128)S(1)}, u32[]{:S(2)}, u32[]{:S(2)}) collective-permute-start(f32[1,2]{1,0:T(1,128)S(1)} %add.284), channel_id=1, source_target_pairs={{0,16},{1,17},{2,18},{3,19},{4,20},{5,21},{6,22},{7,23},{8,24},{9,... | collective-permute-start | bytes 32 | tf_op jit(solution)/shard_map/ppermute | solution.py:54
  316.6 5.1 %collective-permute-start.36 = (f32[1,2]{1,0:T(1,128)S(1)}, f32[1,2]{1,0:T(1,128)S(1)}, u32[]{:S(2)}, u32[]{:S(2)}) collective-permute-start(f32[1,2]{1,0:T(1,128)S(1)} %add.287), channel_id=1, source_target_pairs={{0,4},{1,5},{2,6},{3,7},{4,0},{5,1},{6,2},{7,3},{8,12},{9,13},{10,... | collective-permute-start | bytes 32 | tf_op jit(solution)/shard_map/ppermute | solution.py:54
  325.3 5.1 %collective-permute-start.38 = (f32[1,2]{1,0:T(1,128)S(1)}, f32[1,2]{1,0:T(1,128)S(1)}, u32[]{:S(2)}, u32[]{:S(2)}) collective-permute-start(f32[1,2]{1,0:T(1,128)S(1)} %add.289), channel_id=1, source_target_pairs={{0,16},{1,17},{2,18},{3,19},{4,20},{5,21},{6,22},{7,23},{8,24},{9,... | collective-permute-start | bytes 32 | tf_op jit(solution)/shard_map/ppermute | solution.py:54
  332.4 3.7 collective-permute-start.40
  336.0 5.2 %collective-permute-start.41 = (f32[2,2]{1,0:T(2,128)S(1)}, f32[2,2]{1,0:T(2,128)S(1)}, u32[]{:S(2)}, u32[]{:S(2)}) collective-permute-start(f32[2,2]{1,0:T(2,128)S(1)} %fusion.87), channel_id=1, source_target_pairs={{0,4},{1,5},{2,6},{3,7},{4,0},{5,1},{6,2},{7,3},{8,12},{9,13},{10,... | collective-permute-start | bytes 56 | tf_op jit(solution)/shard_map/ppermute | solution.py:54
  341.2 3.6 collective-permute-start.42
  344.8 5.1 %collective-permute-start.43 = (f32[2,2]{1,0:T(2,128)S(1)}, f32[2,2]{1,0:T(2,128)S(1)}, u32[]{:S(2)}, u32[]{:S(2)}) collective-permute-start(f32[2,2]{1,0:T(2,128)S(1)} %add.294), channel_id=1, source_target_pairs={{0,16},{1,17},{2,18},{3,19},{4,20},{5,21},{6,22},{7,23},{8,24},{9,... | collective-permute-start | bytes 56 | tf_op jit(solution)/shard_map/ppermute | solution.py:54
  351.3 16.2 %collective-permute-start.44 = (bf16[4,2,1,256,256]{4,3,0,1,2:T(8,128)(2,1)S(1)}, bf16[4,2,1,256,256]{4,3,0,1,2:T(8,128)(2,1)S(1)}, u32[]{:S(2)}, u32[]{:S(2)}) collective-permute-start(bf16[4,2,1,256,256]{4,3,0,1,2:T(8,128)(2,1)S(1)} %get-tuple-element.20), channel_id=1, source_target_pairs={{0,1},{1,2},{2,3},{3,4},{4,5},{5,6},{6,7},{7,8},{8,9},{9,10},{10,1... | collective-permute-start | bytes 3145736 | tf_op jit(solution)/shard_map/ppermute | solution.py:16
  353.3 15.9 %collective-permute-start.45 = (bf16[4,2,1,256,256]{4,3,0,1,2:T(8,128)(2,1)S(1)}, bf16[4,2,1,256,256]{4,3,0,1,2:T(8,128)(2,1)S(1)}, u32[]{:S(2)}, u32[]{:S(2)}) collective-permute-start(bf16[4,2,1,256,256]{4,3,0,1,2:T(8,128)(2,1)S(1)} %get-tuple-element.21), channel_id=1, source_target_pairs={{1,0},{2,1},{3,2},{4,3},{5,4},{6,5},{7,6},{8,7},{9,8},{10,9},{11,1... | collective-permute-start | bytes 3145736 | tf_op jit(solution)/shard_map/ppermute | solution.py:17
  455.7 5.1 %collective-permute-start.48 = (f32[1,2]{1,0:T(1,128)S(1)}, f32[1,2]{1,0:T(1,128)S(1)}, u32[]{:S(2)}, u32[]{:S(2)}) collective-permute-start(f32[1,2]{1,0:T(1,128)S(1)} %add.298), channel_id=1, source_target_pairs={{0,4},{1,5},{2,6},{3,7},{4,0},{5,1},{6,2},{7,3},{8,12},{9,13},{10,... | collective-permute-start | bytes 32 | tf_op jit(solution)/shard_map/ppermute | solution.py:54
  464.3 5.1 %collective-permute-start.50 = (f32[1,2]{1,0:T(1,128)S(1)}, f32[1,2]{1,0:T(1,128)S(1)}, u32[]{:S(2)}, u32[]{:S(2)}) collective-permute-start(f32[1,2]{1,0:T(1,128)S(1)} %add.300), channel_id=1, source_target_pairs={{0,16},{1,17},{2,18},{3,19},{4,20},{5,21},{6,22},{7,23},{8,24},{9,... | collective-permute-start | bytes 32 | tf_op jit(solution)/shard_map/ppermute | solution.py:54
  (39 other events, 420.2 us)
Sparse Core Ops, SparseCore 0:
  31.2 81.8 all-reduce.3
  193.8 77.4 all-reduce.5
  371.8 77.3 all-reduce.7
